TPU v7x, 768 devices: a whole 4x8x12 slice. The times are simulated.
768 devices in a mesh: dp: 96 (over y, z), group: 8 (over x, core).
Axes of the slice: x: 4, y: 8, z: 12, core: 2. Of those that a mesh axis runs over, the one named last changes fastest.
Arguments:
- queries: bfloat16 [98304, 2048], P(('dp', 'group')), may hold values from -100 to 100
- key_states: bfloat16 [98304, 512], P(('dp', 'group')), may hold values from -4 to 4
- value_states: bfloat16 [98304, 512], P(('dp', 'group')), may hold values from -6 to 6
- grad_out: bfloat16 [98304, 2048], P(('dp', 'group')), may hold values from -6 to 6
- doc_ids: int32 [98304], P(('dp', 'group')), may hold values from 0 to 145, never falling along the last dimension, each value on 1 to 896 neighbouring positions
Outputs:
- attended: bfloat16 [98304, 2048], P(('dp', 'group'))
- grad_queries: bfloat16 [98304, 2048], P(('dp', 'group'))
- grad_keys: bfloat16 [98304, 512], P(('dp', 'group'))
- grad_values: bfloat16 [98304, 512], P(('dp', 'group'))
Inputs may be any that keep to these rules, and one draw needn't show every extreme that they name: `doc_ids`: ids never fall along the window; every document holds 1 to 896 tokens, and some document exactly 896.
All inputs are finite; a program needn't handle non-finite values.
Results may differ from a plain program's by a relative error of at most 0.02.
Values may be sent and summed in bfloat16 or wider, within the bound.
A program may use at most 32 MiB of HBM per device.

v0:
```python
import jax
import jax.numpy as jnp
from jax import lax
from jax.sharding import PartitionSpec as P

HEADS = 16
KV_HEADS = 4
HEAD = 128
WINDOW = 8


def passed_along(value, axis, steps):
    count = lax.axis_size(axis)
    leading, last = (max(0, -steps), min(count, count - steps))
    return lax.ppermute(value, axis, [(source, source + steps) for source in range(leading, last)])


def head_terms(query_head, key_head, value_head, grad_head, allowed):
    softmax_scale = HEAD ** (-0.5)
    scores = (
        jnp.einsum("igd,jd->gij", query_head, key_head, preferred_element_type=jnp.float32)
        * softmax_scale
    )
    scores = jnp.where(allowed[None], scores, -jnp.inf)
    row_max = jnp.max(scores, axis=-1, keepdims=True)
    log_total = row_max + jnp.log(jnp.sum(jnp.exp(scores - row_max), axis=-1, keepdims=True))
    weights = jnp.where(allowed[None], jnp.exp(scores - log_total), 0.0)
    probs_low = weights.astype(jnp.bfloat16)
    output = jnp.einsum(
        "gij,jd->igd", probs_low, value_head, preferred_element_type=jnp.float32
    ).astype(jnp.bfloat16)
    row_delta = jnp.sum(grad_head.astype(jnp.float32) * output.astype(jnp.float32), axis=-1)
    grad_probs = jnp.einsum(
        "igd,jd->gij", grad_head, value_head, preferred_element_type=jnp.float32
    )
    grad_scores = (weights * (grad_probs - row_delta.T[:, :, None]) * softmax_scale).astype(
        jnp.bfloat16
    )
    grad_query = jnp.einsum(
        "gij,jd->igd", grad_scores, key_head, preferred_element_type=jnp.float32
    ).astype(jnp.bfloat16)
    grad_key = jnp.einsum(
        "gij,igd->jd", grad_scores, query_head, preferred_element_type=jnp.float32
    )
    grad_value = jnp.einsum("gij,igd->jd", probs_low, grad_head, preferred_element_type=jnp.float32)
    return (output, grad_query, grad_key, grad_value)


def local(queries, key_states, value_states, grad_out, doc_ids):
    tok_rows = queries.shape[0]
    groups = HEADS // KV_HEADS
    device_rank = lax.axis_index(("dp", "group"))
    current = (key_states, value_states, doc_ids)
    gathered = [current]
    for distance in range(1, WINDOW):
        current = passed_along((current[0], current[1], current[2]), ("dp", "group"), 1)
        gathered.append(current)
    key_stack = jnp.stack([member[0] for member in gathered], 0)
    value_stack = jnp.stack([member[1] for member in gathered], 0)
    id_stack = jnp.stack([member[2] for member in gathered], 0)
    window_len = WINDOW * tok_rows
    key_index = jnp.arange(window_len, dtype=jnp.int32)
    distance_of = key_index // tok_rows
    key_place = (device_rank - distance_of) * tok_rows + key_index % tok_rows
    query_place = device_rank * tok_rows + jnp.arange(tok_rows, dtype=jnp.int32)
    allowed = (
        (id_stack.reshape(window_len)[None, :] == doc_ids[:, None])
        & (key_place[None, :] <= query_place[:, None])
        & (distance_of <= device_rank)[None, :]
    )
    query_heads = jnp.moveaxis(queries.reshape(tok_rows, KV_HEADS, groups, HEAD), 1, 0)
    grad_heads = jnp.moveaxis(grad_out.reshape(tok_rows, KV_HEADS, groups, HEAD), 1, 0)
    key_heads = jnp.moveaxis(key_stack.reshape(window_len, KV_HEADS, HEAD), 1, 0)
    value_heads = jnp.moveaxis(value_stack.reshape(window_len, KV_HEADS, HEAD), 1, 0)

    def per_head(operands):
        return head_terms(operands[0], operands[1], operands[2], operands[3], allowed)

    output, grad_query, grad_key, grad_value = lax.map(
        per_head, (query_heads, key_heads, value_heads, grad_heads)
    )
    attended = jnp.moveaxis(output, 0, 1).reshape(tok_rows, HEADS * HEAD)
    grad_queries = jnp.moveaxis(grad_query, 0, 1).reshape(tok_rows, HEADS * HEAD)
    key_terms = jnp.moveaxis(grad_key, 0, 1).reshape(WINDOW, tok_rows, KV_HEADS * HEAD)
    value_terms = jnp.moveaxis(grad_value, 0, 1).reshape(WINDOW, tok_rows, KV_HEADS * HEAD)
    totals = (key_terms[WINDOW - 1], value_terms[WINDOW - 1])
    for distance in range(WINDOW - 2, -1, -1):
        arrived = passed_along((totals[0], totals[1]), ("dp", "group"), -1)
        totals = (arrived[0] + key_terms[distance], arrived[1] + value_terms[distance])
    return (attended, grad_queries, totals[0].astype(jnp.bfloat16), totals[1].astype(jnp.bfloat16))


def solution(mesh):
    placed = (
        P(("dp", "group"), None),
        P(("dp", "group"), None),
        P(("dp", "group"), None),
        P(("dp", "group"), None),
        P(("dp", "group")),
    )
    return jax.shard_map(
        local,
        mesh=mesh,
        in_specs=placed,
        out_specs=(
            P(("dp", "group"), None),
            P(("dp", "group"), None),
            P(("dp", "group"), None),
            P(("dp", "group"), None),
        ),
        check_vma=False,
    )
```

profile of v0, /device:TPU:32, one launch (start us, length us, event | category | flops | bytes accessed | tf_op | source)
XLA Modules:
  0.0 278.9 jit_solution(1765898733702631840)
XLA Ops:
  0.6 1.9 collective-permute-start.14
  2.6 3.5 %collective-permute-start = (bf16[128,512]{1,0:T(8,128)(2,1)}, bf16[128,512]{1,0:T(8,128)(2,1)S(1)}, u32[]{:S(2)}, u32[]{:S(2)}) collective-permute-start(bf16[128,512]{1,0:T(8,128)(2,1)} %param.9), channel_id=1, source_target_pairs={{0,1},{1,2},{2,3},{3,4},{4,5},{5,6},{6,7},{7,8},{8,9},{9,10},{10,1... | collective-permute-start | bytes 393224 | tf_op jit(solution)/shard_map/ppermute | solution.py:15
  6.1 1.9 collective-permute-start.7
  9.6 12.4 %collective-permute-done.7 = s32[128]{0:T(128)S(1)} collective-permute-done((s32[128]{0:T(128)}, s32[128]{0:T(128)S(1)}, u32[]{:S(2)}, u32[]{:S(2)}) %collective-permute-start.7) | collective-permute-done | bytes 544 | tf_op jit(solution)/shard_map/ppermute | solution.py:15
  24.8 7.5 %collective-permute-done.8 = s32[128]{0:T(128)S(1)} collective-permute-done((s32[128]{0:T(128)S(1)}, s32[128]{0:T(128)S(1)}, u32[]{:S(2)}, u32[]{:S(2)}) %collective-permute-start.8) | collective-permute-done | bytes 544 | tf_op jit(solution)/shard_map/ppermute | solution.py:15
  34.2 8.4 %collective-permute-done.9 = s32[128]{0:T(128)S(1)} collective-permute-done((s32[128]{0:T(128)S(1)}, s32[128]{0:T(128)S(1)}, u32[]{:S(2)}, u32[]{:S(2)}) %collective-permute-start.9) | collective-permute-done | bytes 544 | tf_op jit(solution)/shard_map/ppermute | solution.py:15
  44.5 8.4 %collective-permute-done.10 = s32[128]{0:T(128)S(1)} collective-permute-done((s32[128]{0:T(128)S(1)}, s32[128]{0:T(128)S(1)}, u32[]{:S(2)}, u32[]{:S(2)}) %collective-permute-start.10) | collective-permute-done | bytes 544 | tf_op jit(solution)/shard_map/ppermute | solution.py:15
  54.8 8.4 %collective-permute-done.11 = s32[128]{0:T(128)S(1)} collective-permute-done((s32[128]{0:T(128)S(1)}, s32[128]{0:T(128)S(1)}, u32[]{:S(2)}, u32[]{:S(2)}) %collective-permute-start.11) | collective-permute-done | bytes 544 | tf_op jit(solution)/shard_map/ppermute | solution.py:15
  65.1 8.4 %collective-permute-done.12 = s32[128]{0:T(128)S(1)} collective-permute-done((s32[128]{0:T(128)S(1)}, s32[128]{0:T(128)S(1)}, u32[]{:S(2)}, u32[]{:S(2)}) %collective-permute-start.12) | collective-permute-done | bytes 544 | tf_op jit(solution)/shard_map/ppermute | solution.py:15
  78.1 5.7 %collective-permute-done.13 = s32[128]{0:T(128)S(1)} collective-permute-done((s32[128]{0:T(128)S(1)}, s32[128]{0:T(128)S(1)}, u32[]{:S(2)}, u32[]{:S(2)}) %collective-permute-start.13) | collective-permute-done | bytes 544 | tf_op jit(solution)/shard_map/ppermute | solution.py:15
  83.9 1.9 collective-permute-start.15
  88.4 7.2 %collective-permute-done.15 = bf16[128,512]{1,0:T(8,128)(2,1)S(1)} collective-permute-done((bf16[128,512]{1,0:T(8,128)(2,1)S(1)}, bf16[128,512]{1,0:T(8,128)(2,1)S(1)}, u32[]{:S(2)}, u32[]{:S(2)}) %collective-permute-start.15) | collective-permute-done | bytes 131104 | tf_op jit(solution)/shard_map/ppermute | solution.py:15
  100.1 7.2 %collective-permute-done.16 = bf16[128,512]{1,0:T(8,128)(2,1)S(1)} collective-permute-done((bf16[128,512]{1,0:T(8,128)(2,1)S(1)}, bf16[128,512]{1,0:T(8,128)(2,1)S(1)}, u32[]{:S(2)}, u32[]{:S(2)}) %collective-permute-start.16) | collective-permute-done | bytes 131104 | tf_op jit(solution)/shard_map/ppermute | solution.py:15
  111.8 7.2 %collective-permute-done.17 = bf16[128,512]{1,0:T(8,128)(2,1)S(1)} collective-permute-done((bf16[128,512]{1,0:T(8,128)(2,1)S(1)}, bf16[128,512]{1,0:T(8,128)(2,1)S(1)}, u32[]{:S(2)}, u32[]{:S(2)}) %collective-permute-start.17) | collective-permute-done | bytes 131104 | tf_op jit(solution)/shard_map/ppermute | solution.py:15
  123.5 7.2 %collective-permute-done.18 = bf16[128,512]{1,0:T(8,128)(2,1)S(1)} collective-permute-done((bf16[128,512]{1,0:T(8,128)(2,1)S(1)}, bf16[128,512]{1,0:T(8,128)(2,1)S(1)}, u32[]{:S(2)}, u32[]{:S(2)}) %collective-permute-start.18) | collective-permute-done | bytes 131104 | tf_op jit(solution)/shard_map/ppermute | solution.py:15
  135.2 7.2 %collective-permute-done.19 = bf16[128,512]{1,0:T(8,128)(2,1)S(1)} collective-permute-done((bf16[128,512]{1,0:T(8,128)(2,1)S(1)}, bf16[128,512]{1,0:T(8,128)(2,1)S(1)}, u32[]{:S(2)}, u32[]{:S(2)}) %collective-permute-start.19) | collective-permute-done | bytes 131104 | tf_op jit(solution)/shard_map/ppermute | solution.py:15
  146.9 7.2 %collective-permute-done.20 = bf16[128,512]{1,0:T(8,128)(2,1)S(1)} collective-permute-done((bf16[128,512]{1,0:T(8,128)(2,1)S(1)}, bf16[128,512]{1,0:T(8,128)(2,1)S(1)}, u32[]{:S(2)}, u32[]{:S(2)}) %collective-permute-start.20) | collective-permute-done | bytes 131104 | tf_op jit(solution)/shard_map/ppermute | solution.py:15
  160.2 28.4 %while.17 = (s32[]{:T(128)}, bf16[4,128,4,128]{1,3,2,0:T(8,128)(2,1)}, bf16[4,128,4,128]{1,3,2,0:T(8,128)(2,1)}, f32[4,1024,128]{2,1,0:T(8,128)}, f32[4,1024,128...) while((s32[]{:T(128)}, ...), condition=%wide.region_4.5_spmd.clone, body=%wide.region_0.4_spmd.clone.sunk | while | flops 815135744 | bytes 21797036 | solution.py:79
  190.4 1.9 collective-permute-start.28
  192.6 2.4 collective-permute-start.21
  196.2 9.2 %collective-permute-start.29 = (f32[128,512]{1,0:T(8,128)S(1)}, f32[128,512]{1,0:T(8,128)S(1)}, u32[]{:S(2)}, u32[]{:S(2)}) collective-permute-start(f32[128,512]{1,0:T(8,128)S(1)} %bitcast_add_fusion.6), channel_id=1, source_target_pairs={{1,0},{2,1},{3,2},{4,3},{5,4},{6,5},{7,6},{8,7},{9,8},{10,9},{11,1... | collective-permute-start | bytes 786440 | tf_op jit(solution)/shard_map/ppermute | solution.py:15
  205.5 2.8 collective-permute-start.22
  209.4 9.2 %collective-permute-start.30 = (f32[128,512]{1,0:T(8,128)S(1)}, f32[128,512]{1,0:T(8,128)S(1)}, u32[]{:S(2)}, u32[]{:S(2)}) collective-permute-start(f32[128,512]{1,0:T(8,128)S(1)} %bitcast_add_fusion.5), channel_id=1, source_target_pairs={{1,0},{2,1},{3,2},{4,3},{5,4},{6,5},{7,6},{8,7},{9,8},{10,9},{11,1... | collective-permute-start | bytes 786440 | tf_op jit(solution)/shard_map/ppermute | solution.py:15
  218.7 2.8 collective-permute-start.23
  222.5 9.2 %collective-permute-start.31 = (f32[128,512]{1,0:T(8,128)S(1)}, f32[128,512]{1,0:T(8,128)S(1)}, u32[]{:S(2)}, u32[]{:S(2)}) collective-permute-start(f32[128,512]{1,0:T(8,128)S(1)} %bitcast_add_fusion.4), channel_id=1, source_target_pairs={{1,0},{2,1},{3,2},{4,3},{5,4},{6,5},{7,6},{8,7},{9,8},{10,9},{11,1... | collective-permute-start | bytes 786440 | tf_op jit(solution)/shard_map/ppermute | solution.py:15
  231.8 2.8 collective-permute-start.24
  235.7 9.4 %collective-permute-start.32 = (f32[128,512]{1,0:T(8,128)S(1)}, f32[128,512]{1,0:T(8,128)S(1)}, u32[]{:S(2)}, u32[]{:S(2)}) collective-permute-start(f32[128,512]{1,0:T(8,128)S(1)} %bitcast_add_fusion.3), channel_id=1, source_target_pairs={{1,0},{2,1},{3,2},{4,3},{5,4},{6,5},{7,6},{8,7},{9,8},{10,9},{11,1... | collective-permute-start | bytes 786440 | tf_op jit(solution)/shard_map/ppermute | solution.py:15
  245.1 2.6 collective-permute-start.25
  249.0 9.4 %collective-permute-start.33 = (f32[128,512]{1,0:T(8,128)S(1)}, f32[128,512]{1,0:T(8,128)S(1)}, u32[]{:S(2)}, u32[]{:S(2)}) collective-permute-start(f32[128,512]{1,0:T(8,128)S(1)} %bitcast_add_fusion.2), channel_id=1, source_target_pairs={{1,0},{2,1},{3,2},{4,3},{5,4},{6,5},{7,6},{8,7},{9,8},{10,9},{11,1... | collective-permute-start | bytes 786440 | tf_op jit(solution)/shard_map/ppermute | solution.py:15
  258.4 2.6 collective-permute-start.26
  262.3 9.2 %collective-permute-start.34 = (f32[128,512]{1,0:T(8,128)S(1)}, f32[128,512]{1,0:T(8,128)S(1)}, u32[]{:S(2)}, u32[]{:S(2)}) collective-permute-start(f32[128,512]{1,0:T(8,128)S(1)} %bitcast_add_fusion.1), channel_id=1, source_target_pairs={{1,0},{2,1},{3,2},{4,3},{5,4},{6,5},{7,6},{8,7},{9,8},{10,9},{11,1... | collective-permute-start | bytes 786440 | tf_op jit(solution)/shard_map/ppermute | solution.py:15
  271.6 2.8 collective-permute-start.27
  (147 shorter events, 89.8 us)
Async XLA Ops:
  0.6 83.2 %collective-permute-start.14 = (bf16[128,512]{1,0:T(8,128)(2,1)}, bf16[128,512]{1,0:T(8,128)(2,1)S(1)}, u32[]{:S(2)}, u32[]{:S(2)}) collective-permute-start(bf16[128,512]{1,0:T(8,128)(2,1)} %param.8), channel_id=1, source_target_pairs={{0,1},{1,2},{2,3},{3,4},{4,5},{5,6},{6,7},{7,8},{8,9},{9,10},{10,1... | collective-permute-start | bytes 393224 | tf_op jit(solution)/shard_map/ppermute | solution.py:15
  2.6 83.9 %collective-permute-start = (bf16[128,512]{1,0:T(8,128)(2,1)}, bf16[128,512]{1,0:T(8,128)(2,1)S(1)}, u32[]{:S(2)}, u32[]{:S(2)}) collective-permute-start(bf16[128,512]{1,0:T(8,128)(2,1)} %param.9), channel_id=1, source_target_pairs={{0,1},{1,2},{2,3},{3,4},{4,5},{5,6},{6,7},{7,8},{8,9},{9,10},{10,1... | collective-permute-start | bytes 393224 | tf_op jit(solution)/shard_map/ppermute | solution.py:15
  6.1 15.9 %collective-permute-start.7 = (s32[128]{0:T(128)}, s32[128]{0:T(128)S(1)}, u32[]{:S(2)}, u32[]{:S(2)}) collective-permute-start(s32[128]{0:T(128)} %param.11), channel_id=1, source_target_pairs={{0,1},{1,2},{2,3},{3,4},{4,5},{5,6},{6,7},{7,8},{8,9},{9,10},{10,1... | collective-permute-start | bytes 1544 | tf_op jit(solution)/shard_map/ppermute | solution.py:15
  22.0 10.3 %collective-permute-start.8 = (s32[128]{0:T(128)S(1)}, s32[128]{0:T(128)S(1)}, u32[]{:S(2)}, u32[]{:S(2)}) collective-permute-start(s32[128]{0:T(128)S(1)} %collective-permute-done.7), channel_id=1, source_target_pairs={{0,1},{1,2},{2,3},{3,4},{4,5},{5,6},{6,7},{7,8},{8,9},{9,10},{10,1... | collective-permute-start | bytes 1544 | tf_op jit(solution)/shard_map/ppermute | solution.py:15
  32.3 10.3 %collective-permute-start.9 = (s32[128]{0:T(128)S(1)}, s32[128]{0:T(128)S(1)}, u32[]{:S(2)}, u32[]{:S(2)}) collective-permute-start(s32[128]{0:T(128)S(1)} %collective-permute-done.8), channel_id=1, source_target_pairs={{0,1},{1,2},{2,3},{3,4},{4,5},{5,6},{6,7},{7,8},{8,9},{9,10},{10,1... | collective-permute-start | bytes 1544 | tf_op jit(solution)/shard_map/ppermute | solution.py:15
  52.9 10.3 %collective-permute-start.11 = (s32[128]{0:T(128)S(1)}, s32[128]{0:T(128)S(1)}, u32[]{:S(2)}, u32[]{:S(2)}) collective-permute-start(s32[128]{0:T(128)S(1)} %collective-permute-done.10), channel_id=1, source_target_pairs={{0,1},{1,2},{2,3},{3,4},{4,5},{5,6},{6,7},{7,8},{8,9},{9,10},{10,1... | collective-permute-start | bytes 1544 | tf_op jit(solution)/shard_map/ppermute | solution.py:15
  63.2 10.3 %collective-permute-start.12 = (s32[128]{0:T(128)S(1)}, s32[128]{0:T(128)S(1)}, u32[]{:S(2)}, u32[]{:S(2)}) collective-permute-start(s32[128]{0:T(128)S(1)} %collective-permute-done.11), channel_id=1, source_target_pairs={{0,1},{1,2},{2,3},{3,4},{4,5},{5,6},{6,7},{7,8},{8,9},{9,10},{10,1... | collective-permute-start | bytes 1544 | tf_op jit(solution)/shard_map/ppermute | solution.py:15
  73.5 10.3 %collective-permute-start.13 = (s32[128]{0:T(128)S(1)}, s32[128]{0:T(128)S(1)}, u32[]{:S(2)}, u32[]{:S(2)}) collective-permute-start(s32[128]{0:T(128)S(1)} %collective-permute-done.12), channel_id=1, source_target_pairs={{0,1},{1,2},{2,3},{3,4},{4,5},{5,6},{6,7},{7,8},{8,9},{9,10},{10,1... | collective-permute-start | bytes 1544 | tf_op jit(solution)/shard_map/ppermute | solution.py:15
  83.9 11.7 %collective-permute-start.15 = (bf16[128,512]{1,0:T(8,128)(2,1)S(1)}, bf16[128,512]{1,0:T(8,128)(2,1)S(1)}, u32[]{:S(2)}, u32[]{:S(2)}) collective-permute-start(bf16[128,512]{1,0:T(8,128)(2,1)S(1)} %collective-permute-done.14), channel_id=1, source_target_pairs={{0,1},{1,2},{2,3},{3,4},{4,5},{5,6},{6,7},{7,8},{8,9},{9,10},{10,1... | collective-permute-start | bytes 393224 | tf_op jit(solution)/shard_map/ppermute | solution.py:15
  86.4 11.7 %collective-permute-start.1 = (bf16[128,512]{1,0:T(8,128)(2,1)S(1)}, bf16[128,512]{1,0:T(8,128)(2,1)S(1)}, u32[]{:S(2)}, u32[]{:S(2)}) collective-permute-start(bf16[128,512]{1,0:T(8,128)(2,1)S(1)} %collective-permute-done), channel_id=1, source_target_pairs={{0,1},{1,2},{2,3},{3,4},{4,5},{5,6},{6,7},{7,8},{8,9},{9,10},{10,1... | collective-permute-start | bytes 393224 | tf_op jit(solution)/shard_map/ppermute | solution.py:15
  95.6 11.7 %collective-permute-start.16 = (bf16[128,512]{1,0:T(8,128)(2,1)S(1)}, bf16[128,512]{1,0:T(8,128)(2,1)S(1)}, u32[]{:S(2)}, u32[]{:S(2)}) collective-permute-start(bf16[128,512]{1,0:T(8,128)(2,1)S(1)} %collective-permute-done.15), channel_id=1, source_target_pairs={{0,1},{1,2},{2,3},{3,4},{4,5},{5,6},{6,7},{7,8},{8,9},{9,10},{10,1... | collective-permute-start | bytes 393224 | tf_op jit(solution)/shard_map/ppermute | solution.py:15
  98.2 11.7 %collective-permute-start.2 = (bf16[128,512]{1,0:T(8,128)(2,1)S(1)}, bf16[128,512]{1,0:T(8,128)(2,1)S(1)}, u32[]{:S(2)}, u32[]{:S(2)}) collective-permute-start(bf16[128,512]{1,0:T(8,128)(2,1)S(1)} %collective-permute-done.1), channel_id=1, source_target_pairs={{0,1},{1,2},{2,3},{3,4},{4,5},{5,6},{6,7},{7,8},{8,9},{9,10},{10,1... | collective-permute-start | bytes 393224 | tf_op jit(solution)/shard_map/ppermute | solution.py:15
  107.3 11.7 %collective-permute-start.17 = (bf16[128,512]{1,0:T(8,128)(2,1)S(1)}, bf16[128,512]{1,0:T(8,128)(2,1)S(1)}, u32[]{:S(2)}, u32[]{:S(2)}) collective-permute-start(bf16[128,512]{1,0:T(8,128)(2,1)S(1)} %collective-permute-done.16), channel_id=1, source_target_pairs={{0,1},{1,2},{2,3},{3,4},{4,5},{5,6},{6,7},{7,8},{8,9},{9,10},{10,1... | collective-permute-start | bytes 393224 | tf_op jit(solution)/shard_map/ppermute | solution.py:15
  109.9 11.7 %collective-permute-start.3 = (bf16[128,512]{1,0:T(8,128)(2,1)S(1)}, bf16[128,512]{1,0:T(8,128)(2,1)S(1)}, u32[]{:S(2)}, u32[]{:S(2)}) collective-permute-start(bf16[128,512]{1,0:T(8,128)(2,1)S(1)} %collective-permute-done.2), channel_id=1, source_target_pairs={{0,1},{1,2},{2,3},{3,4},{4,5},{5,6},{6,7},{7,8},{8,9},{9,10},{10,1... | collective-permute-start | bytes 393224 | tf_op jit(solution)/shard_map/ppermute | solution.py:15
  119.0 11.7 %collective-permute-start.18 = (bf16[128,512]{1,0:T(8,128)(2,1)S(1)}, bf16[128,512]{1,0:T(8,128)(2,1)S(1)}, u32[]{:S(2)}, u32[]{:S(2)}) collective-permute-start(bf16[128,512]{1,0:T(8,128)(2,1)S(1)} %collective-permute-done.17), channel_id=1, source_target_pairs={{0,1},{1,2},{2,3},{3,4},{4,5},{5,6},{6,7},{7,8},{8,9},{9,10},{10,1... | collective-permute-start | bytes 393224 | tf_op jit(solution)/shard_map/ppermute | solution.py:15
  121.6 11.7 %collective-permute-start.4 = (bf16[128,512]{1,0:T(8,128)(2,1)S(1)}, bf16[128,512]{1,0:T(8,128)(2,1)S(1)}, u32[]{:S(2)}, u32[]{:S(2)}) collective-permute-start(bf16[128,512]{1,0:T(8,128)(2,1)S(1)} %collective-permute-done.3), channel_id=1, source_target_pairs={{0,1},{1,2},{2,3},{3,4},{4,5},{5,6},{6,7},{7,8},{8,9},{9,10},{10,1... | collective-permute-start | bytes 393224 | tf_op jit(solution)/shard_map/ppermute | solution.py:15
  130.7 11.7 %collective-permute-start.19 = (bf16[128,512]{1,0:T(8,128)(2,1)S(1)}, bf16[128,512]{1,0:T(8,128)(2,1)S(1)}, u32[]{:S(2)}, u32[]{:S(2)}) collective-permute-start(bf16[128,512]{1,0:T(8,128)(2,1)S(1)} %collective-permute-done.18), channel_id=1, source_target_pairs={{0,1},{1,2},{2,3},{3,4},{4,5},{5,6},{6,7},{7,8},{8,9},{9,10},{10,1... | collective-permute-start | bytes 393224 | tf_op jit(solution)/shard_map/ppermute | solution.py:15
  133.3 11.7 %collective-permute-start.5 = (bf16[128,512]{1,0:T(8,128)(2,1)S(1)}, bf16[128,512]{1,0:T(8,128)(2,1)S(1)}, u32[]{:S(2)}, u32[]{:S(2)}) collective-permute-start(bf16[128,512]{1,0:T(8,128)(2,1)S(1)} %collective-permute-done.4), channel_id=1, source_target_pairs={{0,1},{1,2},{2,3},{3,4},{4,5},{5,6},{6,7},{7,8},{8,9},{9,10},{10,1... | collective-permute-start | bytes 393224 | tf_op jit(solution)/shard_map/ppermute | solution.py:15
  142.4 11.7 %collective-permute-start.20 = (bf16[128,512]{1,0:T(8,128)(2,1)S(1)}, bf16[128,512]{1,0:T(8,128)(2,1)S(1)}, u32[]{:S(2)}, u32[]{:S(2)}) collective-permute-start(bf16[128,512]{1,0:T(8,128)(2,1)S(1)} %collective-permute-done.19), channel_id=1, source_target_pairs={{0,1},{1,2},{2,3},{3,4},{4,5},{5,6},{6,7},{7,8},{8,9},{9,10},{10,1... | collective-permute-start | bytes 393224 | tf_op jit(solution)/shard_map/ppermute | solution.py:15
  145.0 11.7 %collective-permute-start.6 = (bf16[128,512]{1,0:T(8,128)(2,1)S(1)}, bf16[128,512]{1,0:T(8,128)(2,1)S(1)}, u32[]{:S(2)}, u32[]{:S(2)}) collective-permute-start(bf16[128,512]{1,0:T(8,128)(2,1)S(1)} %collective-permute-done.5), channel_id=1, source_target_pairs={{0,1},{1,2},{2,3},{3,4},{4,5},{5,6},{6,7},{7,8},{8,9},{9,10},{10,1... | collective-permute-start | bytes 393224 | tf_op jit(solution)/shard_map/ppermute | solution.py:15
  192.6 12.9 %collective-permute-start.21 = (f32[128,512]{1,0:T(8,128)S(1)}, f32[128,512]{1,0:T(8,128)S(1)}, u32[]{:S(2)}, u32[]{:S(2)}) collective-permute-start(f32[128,512]{1,0:T(8,128)S(1)} %bitcast.244), channel_id=1, source_target_pairs={{1,0},{2,1},{3,2},{4,3},{5,4},{6,5},{7,6},{8,7},{9,8},{10,9},{11,1... | collective-permute-start | bytes 786440 | tf_op jit(solution)/shard_map/ppermute | solution.py:15
  196.2 13.1 %collective-permute-start.29 = (f32[128,512]{1,0:T(8,128)S(1)}, f32[128,512]{1,0:T(8,128)S(1)}, u32[]{:S(2)}, u32[]{:S(2)}) collective-permute-start(f32[128,512]{1,0:T(8,128)S(1)} %bitcast_add_fusion.6), channel_id=1, source_target_pairs={{1,0},{2,1},{3,2},{4,3},{5,4},{6,5},{7,6},{8,7},{9,8},{10,9},{11,1... | collective-permute-start | bytes 786440 | tf_op jit(solution)/shard_map/ppermute | solution.py:15
  205.5 13.1 %collective-permute-start.22 = (f32[128,512]{1,0:T(8,128)S(1)}, f32[128,512]{1,0:T(8,128)S(1)}, u32[]{:S(2)}, u32[]{:S(2)}) collective-permute-start(f32[128,512]{1,0:T(8,128)S(1)} %bitcast_add_fusion.13), channel_id=1, source_target_pairs={{1,0},{2,1},{3,2},{4,3},{5,4},{6,5},{7,6},{8,7},{9,8},{10,9},{11,1... | collective-permute-start | bytes 786440 | tf_op jit(solution)/shard_map/ppermute | solution.py:15
  209.4 13.1 %collective-permute-start.30 = (f32[128,512]{1,0:T(8,128)S(1)}, f32[128,512]{1,0:T(8,128)S(1)}, u32[]{:S(2)}, u32[]{:S(2)}) collective-permute-start(f32[128,512]{1,0:T(8,128)S(1)} %bitcast_add_fusion.5), channel_id=1, source_target_pairs={{1,0},{2,1},{3,2},{4,3},{5,4},{6,5},{7,6},{8,7},{9,8},{10,9},{11,1... | collective-permute-start | bytes 786440 | tf_op jit(solution)/shard_map/ppermute | solution.py:15
  218.7 13.1 %collective-permute-start.23 = (f32[128,512]{1,0:T(8,128)S(1)}, f32[128,512]{1,0:T(8,128)S(1)}, u32[]{:S(2)}, u32[]{:S(2)}) collective-permute-start(f32[128,512]{1,0:T(8,128)S(1)} %bitcast_add_fusion.12), channel_id=1, source_target_pairs={{1,0},{2,1},{3,2},{4,3},{5,4},{6,5},{7,6},{8,7},{9,8},{10,9},{11,1... | collective-permute-start | bytes 786440 | tf_op jit(solution)/shard_map/ppermute | solution.py:15
  222.5 13.1 %collective-permute-start.31 = (f32[128,512]{1,0:T(8,128)S(1)}, f32[128,512]{1,0:T(8,128)S(1)}, u32[]{:S(2)}, u32[]{:S(2)}) collective-permute-start(f32[128,512]{1,0:T(8,128)S(1)} %bitcast_add_fusion.4), channel_id=1, source_target_pairs={{1,0},{2,1},{3,2},{4,3},{5,4},{6,5},{7,6},{8,7},{9,8},{10,9},{11,1... | collective-permute-start | bytes 786440 | tf_op jit(solution)/shard_map/ppermute | solution.py:15
  231.8 13.2 %collective-permute-start.24 = (f32[128,512]{1,0:T(8,128)S(1)}, f32[128,512]{1,0:T(8,128)S(1)}, u32[]{:S(2)}, u32[]{:S(2)}) collective-permute-start(f32[128,512]{1,0:T(8,128)S(1)} %bitcast_add_fusion.11), channel_id=1, source_target_pairs={{1,0},{2,1},{3,2},{4,3},{5,4},{6,5},{7,6},{8,7},{9,8},{10,9},{11,1... | collective-permute-start | bytes 786440 | tf_op jit(solution)/shard_map/ppermute | solution.py:15
  235.7 13.3 %collective-permute-start.32 = (f32[128,512]{1,0:T(8,128)S(1)}, f32[128,512]{1,0:T(8,128)S(1)}, u32[]{:S(2)}, u32[]{:S(2)}) collective-permute-start(f32[128,512]{1,0:T(8,128)S(1)} %bitcast_add_fusion.3), channel_id=1, source_target_pairs={{1,0},{2,1},{3,2},{4,3},{5,4},{6,5},{7,6},{8,7},{9,8},{10,9},{11,1... | collective-permute-start | bytes 786440 | tf_op jit(solution)/shard_map/ppermute | solution.py:15
  245.1 13.2 %collective-permute-start.25 = (f32[128,512]{1,0:T(8,128)S(1)}, f32[128,512]{1,0:T(8,128)S(1)}, u32[]{:S(2)}, u32[]{:S(2)}) collective-permute-start(f32[128,512]{1,0:T(8,128)S(1)} %bitcast_add_fusion.10), channel_id=1, source_target_pairs={{1,0},{2,1},{3,2},{4,3},{5,4},{6,5},{7,6},{8,7},{9,8},{10,9},{11,1... | collective-permute-start | bytes 786440 | tf_op jit(solution)/shard_map/ppermute | solution.py:15
  249.0 13.3 %collective-permute-start.33 = (f32[128,512]{1,0:T(8,128)S(1)}, f32[128,512]{1,0:T(8,128)S(1)}, u32[]{:S(2)}, u32[]{:S(2)}) collective-permute-start(f32[128,512]{1,0:T(8,128)S(1)} %bitcast_add_fusion.2), channel_id=1, source_target_pairs={{1,0},{2,1},{3,2},{4,3},{5,4},{6,5},{7,6},{8,7},{9,8},{10,9},{11,1... | collective-permute-start | bytes 786440 | tf_op jit(solution)/shard_map/ppermute | solution.py:15
  258.4 13.1 %collective-permute-start.26 = (f32[128,512]{1,0:T(8,128)S(1)}, f32[128,512]{1,0:T(8,128)S(1)}, u32[]{:S(2)}, u32[]{:S(2)}) collective-permute-start(f32[128,512]{1,0:T(8,128)S(1)} %bitcast_add_fusion.9), channel_id=1, source_target_pairs={{1,0},{2,1},{3,2},{4,3},{5,4},{6,5},{7,6},{8,7},{9,8},{10,9},{11,1... | collective-permute-start | bytes 786440 | tf_op jit(solution)/shard_map/ppermute | solution.py:15
  262.3 14.1 %collective-permute-start.34 = (f32[128,512]{1,0:T(8,128)S(1)}, f32[128,512]{1,0:T(8,128)S(1)}, u32[]{:S(2)}, u32[]{:S(2)}) collective-permute-start(f32[128,512]{1,0:T(8,128)S(1)} %bitcast_add_fusion.1), channel_id=1, source_target_pairs={{1,0},{2,1},{3,2},{4,3},{5,4},{6,5},{7,6},{8,7},{9,8},{10,9},{11,1... | collective-permute-start | bytes 786440 | tf_op jit(solution)/shard_map/ppermute | solution.py:15
  (12 other events, 188.9 us)
where the time goes:
time: 280 us; the launch traced here: 279 us
  starting transfers between devices  118 us (42%)
  waiting for transfers between devices  111 us (40%)
  matrix products  23.3 us (8%)
  local copies, waits for them, and re-layouts  18.9 us (7%)
  other arithmetic  6.68 us (2%)
    ppermute x35, starting transfers between devices, passed_along(): lax.ppermute(value, axis, [(source, source + steps) for source in range(l...  118 us
    ppermute x35, waiting for transfers between devices, passed_along(): lax.ppermute(value, axis, [(source, source + steps) for source in range(l...  111 us
    unnamed x28, local copies, waits for them, and re-layouts  11.1 us
  transfers between devices with their start and end apart: 35, of which 21 were waited for; matrix products, arithmetic and copies ran while one was open for 5% of the time, Pallas kernels for 0%

commit v1 on v0

v1 whole, which is shorter than its diff:
```python
import functools

import jax
import jax.numpy as jnp
from jax import lax
from jax.experimental import pallas as pl
from jax.experimental.pallas import tpu as pltpu
from jax.sharding import PartitionSpec as P

MESH = pl.DeviceIdType.MESH
BF16, F32 = jnp.bfloat16, jnp.float32
SCALE = 128 ** -0.5
LOG2E = 1.4426950408889634
BIG = -1e30


def nt(a, b):
    return lax.dot_general(a, b, (((1,), (1,)), ((), ())), preferred_element_type=F32)


def nn(a, b):
    return lax.dot_general(a, b, (((1,), (0,)), ((), ())), preferred_element_type=F32)


def tn(a, b):
    return lax.dot_general(a, b, (((0,), (0,)), ((), ())), preferred_element_type=F32)


def kernel(
    rows_dp, q_in, k_in, v_in, g_in, ids_in, o_out, dq_out, dk_out, dv_out,
    Q, G, K, V, IDS, BIAS, PF, PR, DS, OB, ACC, SND, RCV, OWN, SIB, FIN,
    own_sem, gs_sem, gr_sem, ql_sem, qs_sem, qr_sem,
    rs_sem, rr_sem, ol_sem, os_sem, or_sem, fl_sem, fs_sem, fr_sem,
):
    dp, group = lax.axis_index("dp"), lax.axis_index("group")
    x, k = group // 2, group % 2
    odd = x % 2
    last, first = x // 3, (3 - x) // 3
    nxt, prv = (dp + 1) % rows_dp, (dp + rows_dp - 1) % rows_dp
    sib = (dp, x * 2 + 1 - k)

    def along(step):
        return (dp, ((x + step) % 4) * 2 + k)

    z_next, z_prev = (nxt, group), (prv, group)
    partner_k = (dp, ((x + 1 + 2 * odd) % 4) * 2 + k)
    partner_v = ((dp + last + rows_dp - first) % rows_dp, ((x + 3 + 2 * odd) % 4) * 2 + k)
    relay_k, relay_v = 3 - 2 * odd, 1 + 2 * odd

    def spot(m, pos, core):
        if m == 0:
            return IDS.at[pos, core]
        buf = K if m % 2 else V
        return buf.at[(m - 1) // 2, pl.ds(pl.multiple_of(pos * 256 + core * 128, 128), 128), :]

    def source(m, core):
        if m == 0:
            return ids_in
        arr = k_in if m % 2 else v_in
        return arr.at[:, pl.ds(pl.multiple_of((2 * core + (m - 1) // 2) * 128, 128), 128)]

    def remote(src, dst, send, recv, dev):
        return pltpu.make_async_remote_copy(
            src_ref=src, dst_ref=dst, send_sem=send, recv_sem=recv, device_id=dev, device_id_type=MESH
        )

    def own_copy(m):
        return pltpu.make_async_copy(source(m, k), spot(m, 4, k), own_sem.at[m])

    def sib_send(m):
        return remote(source(m, 1 - k), spot(m, 4, k), gs_sem.at[m, 4, 0], gr_sem.at[m, 4, 0], sib)

    def sib_wait(m):
        remote(source(m, k), spot(m, 4, 1 - k), gs_sem.at[m, 4, 0], gr_sem.at[m, 4, 0], sib).wait_recv()

    def send_own(m, pos, dev):
        for n, core in enumerate((k, 1 - k)):
            target = (dev[0], dev[1] - k + core)
            remote(source(m, core), spot(m, pos, k), gs_sem.at[m, pos, n], gr_sem.at[m, pos, k], target).start()

    def edge(m, src_pos, pos, dev, part):
        return remote(
            spot(m, src_pos, part), spot(m, pos, part), gs_sem.at[m, pos, part], gr_sem.at[m, pos, part], dev
        )

    def arrived(m, pos):
        for part in range(2):
            edge(m, pos, pos, sib, part).wait_recv()

    msgs = range(5)
    for m in msgs:
        own_copy(m).start()
    half_q = pl.ds(pl.multiple_of(k * 1024, 1024), 1024)
    half_s = pl.ds(pl.multiple_of((1 - k) * 1024, 1024), 1024)
    q_own = [
        pltpu.make_async_copy(arr.at[:, half_q], buf.at[k], ql_sem.at[i])
        for i, (arr, buf) in enumerate(((q_in, Q), (g_in, G)))
    ]
    q_send = [
        remote(arr.at[:, half_s], buf.at[k], qs_sem.at[i], qr_sem.at[i], sib)
        for i, (arr, buf) in enumerate(((q_in, Q), (g_in, G)))
    ]
    q_recv = [
        remote(arr.at[:, half_q], buf.at[1 - k], qs_sem.at[i], qr_sem.at[i], sib)
        for i, (arr, buf) in enumerate(((q_in, Q), (g_in, G)))
    ]
    for copy in q_own:
        copy.start()

    barrier = pltpu.get_barrier_semaphore()
    for dev in (sib, along(1), along(2), along(3), z_next, z_prev, partner_v):
        pl.semaphore_signal(barrier, inc=1, device_id=dev, device_id_type=MESH)
    for dev in (along(1), along(3), z_next, z_prev):
        other = (dev[0], dev[1] + 1 - 2 * k)
        pl.semaphore_signal(barrier, inc=1, device_id=other, device_id_type=MESH)
    pl.semaphore_wait(barrier, 11)

    for m in msgs:
        send_own(m, 0, z_next)
        sib_send(m).start()

        @pl.when(x < 3)
        def _():
            send_own(m, 3, along(1))

        @pl.when(x == 0)
        def _():
            send_own(m, 1, along(3))

    for copy in q_send:
        copy.start()

    def forward(m):
        for part in range(2):
            edge(m, 0, 0, sib, part).wait_recv()

            @pl.when(x == 3)
            def _():
                edge(m, 0, 3, along(1), part).start()

            @pl.when(x > 0)
            def _():
                edge(m, 0, 1, along(3), part).start()

    def relay_pos(m):
        return relay_k if m % 2 or m == 0 else relay_v

    def relay(m):
        for part in range(2):
            edge(m, relay_pos(m), relay_pos(m), sib, part).wait_recv()
            edge(m, relay_pos(m), 2, partner_k if m % 2 or m == 0 else partner_v, part).start()

    def complete(m):
        own_copy(m).wait()
        sib_wait(m)
        arrived(m, 4 - relay_pos(m))
        arrived(m, 2)

    for m in (0, 1, 2):
        forward(m)
    relay(0)
    forward(3)
    relay(1)
    forward(4)
    relay(2)
    complete(0)

    chip = 4 * dp + x
    col = lax.broadcasted_iota(jnp.int32, (128, 1024), 1)
    row = lax.broadcasted_iota(jnp.int32, (128, 1024), 0)
    ids = [IDS[b // 2, b % 2] for b in range(10)]
    for t in range(2):
        key_ids = jnp.broadcast_to(jnp.concatenate(ids[1 + t : 9 + t], 1), (128, 1024))
        own_ids = jnp.transpose(jnp.broadcast_to(ids[8 + t], (128, 128)))
        query_ids = jnp.concatenate([own_ids] * 8, 1)
        allowed = (key_ids == query_ids) & (col <= row + 896) & (col >= 128 * (7 - t - 2 * chip))
        BIAS[t] = jnp.where(allowed, 0.0, BIG)
    for copy in q_own:
        copy.wait()
    for copy in q_recv:
        copy.wait_recv()

    def heads_of(ref, t, h):
        return jnp.concatenate([ref[t, :, (4 * h + i) * 128 : (4 * h + i + 1) * 128] for i in range(4)], 0)

    def weigh(h, t):
        lo = 128 * (1 + t)
        scores = nt(heads_of(Q, t, h), K[h, lo : lo + 1024, :]) * (SCALE * LOG2E)
        scores = scores + jnp.concatenate([BIAS[t]] * 4, 0)
        exps = jnp.exp2(scores - jnp.max(scores, -1, keepdims=True))
        probs = exps * (1.0 / jnp.sum(exps, -1, keepdims=True))
        PF[t] = probs
        PR[t, :, lo : lo + 1024] = probs.astype(BF16)

    def attend(h, t):
        lo = 128 * (1 + t)
        keys, values = K[h, lo : lo + 1024, :], V[h, lo : lo + 1024, :]
        g = heads_of(G, t, h)
        out = nn(PR[t, :, lo : lo + 1024], values).astype(BF16)
        delta = jnp.sum(g.astype(F32) * out.astype(F32), -1, keepdims=True)
        grads = (PF[t] * (nt(g, values) - delta)).astype(BF16)
        DS[t, :, lo : lo + 1024] = grads
        dq = (nn(grads, keys) * SCALE).astype(BF16)
        for i in range(4):
            OB[0, h, t, :, i * 128 : (i + 1) * 128] = out[i * 128 : (i + 1) * 128]
            OB[1, h, t, :, i * 128 : (i + 1) * 128] = dq[i * 128 : (i + 1) * 128]
        for n, arr in enumerate((o_out, dq_out)):

            @pl.when(k == t)
            def _():
                out_local(n, arr, h, t).start()

            @pl.when(k != t)
            def _():
                out_remote(n, arr, h, t, k).start()

    def wide(h, core):
        return pl.ds(pl.multiple_of((2 * core + h) * 512, 512), 512)

    def out_local(n, arr, h, t):
        return pltpu.make_async_copy(OB.at[n, h, t], arr.at[:, wide(h, k)], ol_sem.at[n, h])

    def out_remote(n, arr, h, t, core):
        return remote(OB.at[n, h, t], arr.at[:, wide(h, core)], os_sem.at[n, h], or_sem.at[n, h], sib)

    def send_part(n, pos, part, dev):
        return remote(
            SND.at[n, pos, part], RCV.at[n, pos, part], rs_sem.at[n, pos, part], rr_sem.at[n, pos, part], dev
        )

    def send_back(n, part, core):
        dev = (prv, x * 2 + part)
        return remote(SND.at[n, 0, part], RCV.at[n, 0, core], rs_sem.at[n, 0, part], rr_sem.at[n, 0, core], dev)

    def send_sib(n):
        return remote(SIB.at[n, 0], SIB.at[n, 1], fs_sem.at[n], fr_sem.at[n], sib)

    def part_wait(n, pos, part):
        send_part(n, pos, part, sib).wait_recv()

    def fold_pos(n):
        return relay_k if n % 2 else relay_v

    def ship(n, pos, dev):
        for part in range(2):
            SND[n, pos, part] = ACC[n, pos, :, part * 128 : (part + 1) * 128].astype(BF16)
            send_part(n, pos, part, dev).start()

    def partials(n):
        h = n // 2
        left, right, scale = (Q, DS, SCALE) if n % 2 else (G, PR, 1.0)
        a0, a1 = heads_of(left, 0, h), heads_of(left, 1, h)

        def term(t, lo, hi):
            return tn(a1 if t else a0, right[t, :, lo:hi]) * scale

        for pos in (2, 1, 3):
            ACC[n, pos] = term(0, pos * 256, pos * 256 + 256) + term(1, pos * 256, pos * 256 + 256)
            if pos == 2:
                ship(n, 2, along(2) if n == 3 else (partner_k if n % 2 else partner_v))
            elif n == 3:
                ship(n, pos, along(pos))
        if n < 3:
            ship(n, 4 - fold_pos(n), along(4 - fold_pos(n)))
        ACC[n, 0, :, :128] = jnp.zeros((128, 128), F32)
        ACC[n, 0, :, 128:] = term(0, 128, 256)
        ACC[n, 4, :, :128] = term(0, 1024, 1152) + term(1, 1024, 1152)
        ACC[n, 4, :, 128:] = term(1, 1152, 1280)

    def fold(n):
        pos = fold_pos(n)
        for part in range(2):
            part_wait(n, 2, part)
            total = ACC[n, pos, :, part * 128 : (part + 1) * 128] + RCV[n, 2, part].astype(F32)
            SND[n, pos, part] = total.astype(BF16)
            send_part(n, pos, part, along(pos)).start()

    def split(n):
        for part in range(2):
            cols = slice(part * 128, (part + 1) * 128)
            part_wait(n, 1, part)
            part_wait(n, 3, part)
            ahead, behind = RCV[n, 3, part].astype(F32), RCV[n, 1, part].astype(F32)
            zero = jnp.zeros_like(ahead)
            to_prev = ACC[n, 0, :, cols] + jnp.where(x == 3, ahead, zero) + jnp.where(x > 0, behind, zero)
            mine = ACC[n, 4, :, cols] + jnp.where(x < 3, ahead, zero) + jnp.where(x == 0, behind, zero)
            if n == 3:
                part_wait(n, 2, part)
                across = RCV[n, 2, part].astype(F32)
                to_prev = to_prev + jnp.where(x >= 2, across, zero)
                mine = mine + jnp.where(x < 2, across, zero)
            SND[n, 0, part] = to_prev.astype(BF16)
            send_back(n, part, k).start()
            OWN[n, part] = mine
        SIB[n, 0] = OWN[n, 1 - k].astype(BF16)
        send_sib(n).start()

    def narrow(n, core):
        return pl.ds(pl.multiple_of((2 * core + n // 2) * 128, 128), 128)

    def fin_local(n, side):
        core = 1 - k if side else k
        return pltpu.make_async_copy(
            FIN.at[n, side], (dk_out if n % 2 else dv_out).at[:, narrow(n, core)], fl_sem.at[n, side]
        )

    def finish(n):
        remote(SND.at[n, 0, 0], RCV.at[n, 0, k], rs_sem.at[n, 0, 0], rr_sem.at[n, 0, k], sib).wait_recv()
        FIN[n, 0] = jnp.transpose(OWN[n, k] + RCV[n, 0, k].astype(F32)).astype(BF16)
        fin_local(n, 0).start()
        remote(SND.at[n, 0, 0], RCV.at[n, 0, 1 - k], rs_sem.at[n, 0, 0], rr_sem.at[n, 0, 1 - k], sib).wait_recv()
        send_sib(n).wait_recv()
        FIN[n, 1] = jnp.transpose(SIB[n, 1].astype(F32) + RCV[n, 0, 1 - k].astype(F32)).astype(BF16)
        fin_local(n, 1).start()

    complete(1)
    weigh(0, 0)
    relay(3)
    weigh(0, 1)
    partials(0)
    relay(4)
    complete(2)
    attend(0, 0)
    attend(0, 1)
    partials(1)
    complete(3)
    weigh(1, 0)
    fold(0)
    weigh(1, 1)
    partials(2)
    complete(4)
    fold(1)
    attend(1, 0)
    split(0)
    attend(1, 1)
    fold(2)
    partials(3)
    split(1)
    finish(0)
    split(2)
    finish(1)
    split(3)
    finish(2)
    finish(3)

    for n in range(4):
        send_sib(n).wait_send()
        for part in range(2):
            fin_local(n, part).wait()
            for pos in range(4):
                send_part(n, pos, part, sib).wait_send()
    for n, arr in enumerate((o_out, dq_out)):
        for h in range(2):
            out_local(n, arr, h, k).wait()
            out_remote(n, arr, h, 1 - k, k).wait_send()
            out_remote(n, arr, h, 1 - k, 1 - k).wait_recv()
    for copy in q_send:
        copy.wait_send()
    for m in msgs:
        sib_send(m).wait_send()
        for pos in range(4):
            for part in range(2):
                edge(m, pos, pos, sib, part).wait_send()


def put_out(*refs):
    copies = [pltpu.make_async_copy(refs[i], refs[4 + i], refs[8].at[i]) for i in range(4)]
    for copy in copies:
        copy.start()
    for copy in copies:
        copy.wait()


def solution(mesh):
    rows_dp = mesh.shape["dp"]

    def local(queries, key_states, value_states, grad_out, doc_ids):
        hbm, place = pl.BlockSpec(memory_space=pltpu.HBM), pl.BlockSpec(memory_space=pl.ANY)
        dma, vmem = pltpu.SemaphoreType.DMA, pltpu.VMEM
        shapes = tuple(jax.ShapeDtypeStruct((128, width), BF16) for width in (2048, 2048, 512, 512))
        made = pl.pallas_call(
            functools.partial(kernel, rows_dp),
            out_shape=shapes,
            in_specs=[hbm] * 5,
            out_specs=(place,) * 4,
            scratch_shapes=[
                vmem((2, 128, 1024), BF16),
                vmem((2, 128, 1024), BF16),
                vmem((2, 1280, 128), BF16),
                vmem((2, 1280, 128), BF16),
                vmem((5, 2, 1, 128), jnp.int32),
                vmem((2, 128, 1024), F32),
                vmem((2, 512, 1024), F32),
                vmem((2, 512, 1280), BF16),
                vmem((2, 512, 1280), BF16),
                vmem((2, 2, 2, 128, 512), BF16),
                vmem((4, 5, 128, 256), F32),
                vmem((4, 4, 2, 128, 128), BF16),
                vmem((4, 4, 2, 128, 128), BF16),
                vmem((4, 2, 128, 128), F32),
                vmem((4, 2, 128, 128), BF16),
                vmem((4, 2, 128, 128), BF16),
                dma((5,)),
                dma((5, 5, 2)),
                dma((5, 5, 2)),
                dma((2,)),
                dma((2,)),
                dma((2,)),
                dma((4, 4, 2)),
                dma((4, 4, 2)),
                dma((2, 2)),
                dma((2, 2)),
                dma((2, 2)),
                dma((4, 2)),
                dma((4,)),
                dma((4,)),
            ],
            compiler_params=pltpu.CompilerParams(
                collective_id=0, has_side_effects=True, vmem_limit_bytes=48 * 1024 * 1024
            ),
        )(*[pltpu.with_memory_space_constraint(z, pltpu.HBM) for z in (queries, key_states, value_states, grad_out, doc_ids.reshape(1, 128))])
        return pl.pallas_call(
            put_out,
            out_shape=shapes,
            in_specs=[place] * 4,
            out_specs=(hbm,) * 4,
            scratch_shapes=[dma((4,))],
            compiler_params=pltpu.CompilerParams(vmem_limit_bytes=1024 * 1024),
        )(*made)

    row, flat = P(("dp", "group"), None), P(("dp", "group"))
    return jax.shard_map(
        local,
        mesh=mesh,
        in_specs=(row, row, row, row, flat),
        out_specs=(row,) * 4,
        check_vma=False,
    )
```

time: 280 us -> 56.1 us (0.20)
  the two profiles are of different devices: /device:TPU:32 before, /device:TPU:1 now
where the time goes in v1:
time: 56.1 us; the launch traced here: 56 us
  Pallas kernels  55.3 us (99%)
  between operations  0.64 us (1%)
    pallas_call x1, Pallas kernels, local(): pl.pallas_call(functools.partial(kernel, rows_dp), out_shape=shapes, in_s...  54.2 us

profile of v1, /device:TPU:1, one launch (start us, length us, event | category | flops | bytes accessed | tf_op | source)
XLA Modules:
  0.0 56.0 jit_solution(7093200200756616691)
XLA Ops:
  0.6 54.2 %shard_map.84 = (bf16[128,2048]{1,0:T(8,128)(2,1)S(1)}, bf16[128,2048]{1,0:T(8,128)(2,1)S(1)}, bf16[128,512]{1,0:T(8,128)(2,1)S(1)}, bf16[128,512]{1,0:T(8,128)(2,1)S(1)}) custom-call(bf16[128,2048]{1,0:T(8,128)(2,1)} %q_in.1, bf16[128,512]{1,0:T(8,128)(2,1)} %k_in.1, bf16[128,512]{1,0:T(8,128)(2,1)} %v_in.1, bf16[128,2048]{1,0:T(8,128)(2,1)} %g_in.1, ...), custom_call_target="tpu_custom_call" | custom-call | tf_op jit(solution)/shard_map/pallas_call | solution.py:381
  54.9 1.1 %shard_map.85 = (bf16[128,2048]{1,0:T(8,128)(2,1)}, bf16[128,2048]{1,0:T(8,128)(2,1)}, bf16[128,512]{1,0:T(8,128)(2,1)}, bf16[128,512]{1,0:T(8,128)(2,1)}) custom-call(bf16[128,2048]{1,0:T(8,128)(2,1)S(1)} %get-tuple-element.8.refs_0_, bf16[128,2048]{1,0:T(8,128)(2,1)S(1)} %get-tuple-element.9.refs_1_, bf16[128,512]{1,0:T(8,128)(2,1)S(1)} %get-tuple-element.10.refs_2_, ...), custom_call_target="tpu_custom_call" | custom-call | tf_op jit(solution)/shard_map/pallas_call | solution.py:422

commit v2 on v1

--- a/solution.py
+++ b/solution.py
@@ -43,9 +43,11 @@
         return (dp, ((x + step) % 4) * 2 + k)
 
     z_next, z_prev = (nxt, group), (prv, group)
-    partner_k = (dp, ((x + 1 + 2 * odd) % 4) * 2 + k)
-    partner_v = ((dp + last + rows_dp - first) % rows_dp, ((x + 3 + 2 * odd) % 4) * 2 + k)
-    relay_k, relay_v = 3 - 2 * odd, 1 + 2 * odd
+    partner = (
+        (dp, ((x + 1 + 2 * odd) % 4) * 2 + k),
+        ((dp + last + rows_dp - first) % rows_dp, ((x + 3 + 2 * odd) % 4) * 2 + k),
+    )
+    relay_pos = (3 - 2 * odd, 1 + 2 * odd)
 
     def spot(m, pos, core):
         if m == 0:
@@ -87,6 +89,12 @@
         for part in range(2):
             edge(m, pos, pos, sib, part).wait_recv()
 
+    barrier = pltpu.get_barrier_semaphore()
+    for dev in (sib, along(1), along(2), along(3), z_next, z_prev, partner[1]):
+        pl.semaphore_signal(barrier, inc=1, device_id=dev, device_id_type=MESH)
+    for dev in (along(1), along(3), z_next, z_prev):
+        other = (dev[0], dev[1] + 1 - 2 * k)
+        pl.semaphore_signal(barrier, inc=1, device_id=other, device_id_type=MESH)
     msgs = range(5)
     for m in msgs:
         own_copy(m).start()
@@ -107,16 +115,11 @@
     for copy in q_own:
         copy.start()
 
-    barrier = pltpu.get_barrier_semaphore()
-    for dev in (sib, along(1), along(2), along(3), z_next, z_prev, partner_v):
-        pl.semaphore_signal(barrier, inc=1, device_id=dev, device_id_type=MESH)
-    for dev in (along(1), along(3), z_next, z_prev):
-        other = (dev[0], dev[1] + 1 - 2 * k)
-        pl.semaphore_signal(barrier, inc=1, device_id=other, device_id_type=MESH)
     pl.semaphore_wait(barrier, 11)
 
     for m in msgs:
         send_own(m, 0, z_next)
+    for m in msgs:
         sib_send(m).start()
 
         @pl.when(x < 3)
@@ -142,19 +145,18 @@
             def _():
                 edge(m, 0, 1, along(3), part).start()
 
-    def relay_pos(m):
-        return relay_k if m % 2 or m == 0 else relay_v
-
     def relay(m):
         for part in range(2):
-            edge(m, relay_pos(m), relay_pos(m), sib, part).wait_recv()
-            edge(m, relay_pos(m), 2, partner_k if m % 2 or m == 0 else partner_v, part).start()
+            pos = relay_pos[part]
+            edge(m, pos, pos, sib, part).wait_recv()
+            edge(m, pos, 2, partner[part], part).start()
 
     def complete(m):
         own_copy(m).wait()
         sib_wait(m)
-        arrived(m, 4 - relay_pos(m))
-        arrived(m, 2)
+        for part in range(2):
+            edge(m, 4 - relay_pos[part], 4 - relay_pos[part], sib, part).wait_recv()
+            edge(m, 2, 2, sib, part).wait_recv()
 
     for m in (0, 1, 2):
         forward(m)
@@ -192,27 +194,31 @@
         PF[t] = probs
         PR[t, :, lo : lo + 1024] = probs.astype(BF16)
 
+    def put(n, h, t, value):
+        for i in range(4):
+            OB[n, h, t, :, i * 128 : (i + 1) * 128] = value[i * 128 : (i + 1) * 128]
+        arr = (o_out, dq_out)[n]
+
+        @pl.when(k == t)
+        def _():
+            out_local(n, arr, h, t).start()
+
+        @pl.when(k != t)
+        def _():
+            out_remote(n, arr, h, t, k).start()
+
     def attend(h, t):
         lo = 128 * (1 + t)
-        keys, values = K[h, lo : lo + 1024, :], V[h, lo : lo + 1024, :]
+        values = V[h, lo : lo + 1024, :]
         g = heads_of(G, t, h)
         out = nn(PR[t, :, lo : lo + 1024], values).astype(BF16)
         delta = jnp.sum(g.astype(F32) * out.astype(F32), -1, keepdims=True)
-        grads = (PF[t] * (nt(g, values) - delta)).astype(BF16)
-        DS[t, :, lo : lo + 1024] = grads
-        dq = (nn(grads, keys) * SCALE).astype(BF16)
-        for i in range(4):
-            OB[0, h, t, :, i * 128 : (i + 1) * 128] = out[i * 128 : (i + 1) * 128]
-            OB[1, h, t, :, i * 128 : (i + 1) * 128] = dq[i * 128 : (i + 1) * 128]
-        for n, arr in enumerate((o_out, dq_out)):
-
-            @pl.when(k == t)
-            def _():
-                out_local(n, arr, h, t).start()
-
-            @pl.when(k != t)
-            def _():
-                out_remote(n, arr, h, t, k).start()
+        DS[t, :, lo : lo + 1024] = (PF[t] * (nt(g, values) - delta)).astype(BF16)
+        put(0, h, t, out)
+
+    def query_grads(h, t):
+        lo = 128 * (1 + t)
+        put(1, h, t, (nn(DS[t, :, lo : lo + 1024], K[h, lo : lo + 1024, :]) * SCALE).astype(BF16))
 
     def wide(h, core):
         return pl.ds(pl.multiple_of((2 * core + h) * 512, 512), 512)
@@ -238,13 +244,9 @@
     def part_wait(n, pos, part):
         send_part(n, pos, part, sib).wait_recv()
 
-    def fold_pos(n):
-        return relay_k if n % 2 else relay_v
-
-    def ship(n, pos, dev):
-        for part in range(2):
-            SND[n, pos, part] = ACC[n, pos, :, part * 128 : (part + 1) * 128].astype(BF16)
-            send_part(n, pos, part, dev).start()
+    def ship(n, pos, part, dev):
+        SND[n, pos, part] = ACC[n, pos, :, part * 128 : (part + 1) * 128].astype(BF16)
+        send_part(n, pos, part, dev).start()
 
     def partials(n):
         h = n // 2
@@ -256,20 +258,22 @@
 
         for pos in (2, 1, 3):
             ACC[n, pos] = term(0, pos * 256, pos * 256 + 256) + term(1, pos * 256, pos * 256 + 256)
-            if pos == 2:
-                ship(n, 2, along(2) if n == 3 else (partner_k if n % 2 else partner_v))
-            elif n == 3:
-                ship(n, pos, along(pos))
+            for part in range(2):
+                if pos == 2:
+                    ship(n, 2, part, along(2) if n == 3 else partner[part])
+                elif n == 3:
+                    ship(n, pos, part, along(pos))
         if n < 3:
-            ship(n, 4 - fold_pos(n), along(4 - fold_pos(n)))
+            for part in range(2):
+                ship(n, 4 - relay_pos[part], part, along(4 - relay_pos[part]))
         ACC[n, 0, :, :128] = jnp.zeros((128, 128), F32)
         ACC[n, 0, :, 128:] = term(0, 128, 256)
         ACC[n, 4, :, :128] = term(0, 1024, 1152) + term(1, 1024, 1152)
         ACC[n, 4, :, 128:] = term(1, 1152, 1280)
 
     def fold(n):
-        pos = fold_pos(n)
-        for part in range(2):
+        for part in range(2):
+            pos = relay_pos[part]
             part_wait(n, 2, part)
             total = ACC[n, pos, :, part * 128 : (part + 1) * 128] + RCV[n, 2, part].astype(F32)
             SND[n, pos, part] = total.astype(BF16)
@@ -323,23 +327,27 @@
     attend(0, 0)
     attend(0, 1)
     partials(1)
+    query_grads(0, 0)
+    query_grads(0, 1)
     complete(3)
     weigh(1, 0)
     fold(0)
     weigh(1, 1)
     partials(2)
     complete(4)
+    attend(1, 0)
+    attend(1, 1)
     fold(1)
-    attend(1, 0)
+    partials(3)
     split(0)
-    attend(1, 1)
     fold(2)
-    partials(3)
+    query_grads(1, 0)
+    query_grads(1, 1)
+    finish(0)
     split(1)
-    finish(0)
     split(2)
+    split(3)
     finish(1)
-    split(3)
     finish(2)
     finish(3)
 

time: 56.1 us -> 54.9 us (0.979)
  Pallas kernels: 55.3 us -> 54.1 us
    pallas_call x1, Pallas kernels: 54.2 us -> 53 us  [local(): pl.pallas_call(functools.partial(kernel, rows_dp), out_shape=shapes, in_s...]
where the time goes in v2:
time: 54.9 us; the launch traced here: 54.7 us
  Pallas kernels  54.1 us (99%)
  between operations  0.64 us (1%)
    pallas_call x1, Pallas kernels, local(): pl.pallas_call(functools.partial(kernel, rows_dp), out_shape=shapes, in_s...  53 us

profile of v2, /device:TPU:1, one launch (start us, length us, event | category | flops | bytes accessed | tf_op | source)
XLA Modules:
  0.0 54.7 jit_solution(7512745110155111133)
XLA Ops:
  0.6 53.0 %shard_map.84 = (bf16[128,2048]{1,0:T(8,128)(2,1)S(1)}, bf16[128,2048]{1,0:T(8,128)(2,1)S(1)}, bf16[128,512]{1,0:T(8,128)(2,1)S(1)}, bf16[128,512]{1,0:T(8,128)(2,1)S(1)}) custom-call(bf16[128,2048]{1,0:T(8,128)(2,1)} %q_in.1, bf16[128,512]{1,0:T(8,128)(2,1)} %k_in.1, bf16[128,512]{1,0:T(8,128)(2,1)} %v_in.1, bf16[128,2048]{1,0:T(8,128)(2,1)} %g_in.1, ...), custom_call_target="tpu_custom_call" | custom-call | tf_op jit(solution)/shard_map/pallas_call | solution.py:389
  53.6 1.1 %shard_map.85 = (bf16[128,2048]{1,0:T(8,128)(2,1)}, bf16[128,2048]{1,0:T(8,128)(2,1)}, bf16[128,512]{1,0:T(8,128)(2,1)}, bf16[128,512]{1,0:T(8,128)(2,1)}) custom-call(bf16[128,2048]{1,0:T(8,128)(2,1)S(1)} %get-tuple-element.8.refs_0_, bf16[128,2048]{1,0:T(8,128)(2,1)S(1)} %get-tuple-element.9.refs_1_, bf16[128,512]{1,0:T(8,128)(2,1)S(1)} %get-tuple-element.10.refs_2_, ...), custom_call_target="tpu_custom_call" | custom-call | tf_op jit(solution)/shard_map/pallas_call | solution.py:430
